TPU v7x, 128 devices: a whole 4x4x4 slice. The times are simulated.
128 devices in a mesh: row: 8 (over y, core), col: 16 (over x, z).
Axes of the slice: x: 4, y: 4, z: 4, core: 2. Of those that a mesh axis runs over, the one named last changes fastest.
Arguments:
- valence_bands: bfloat16 [256, 96, 9216], P(('row', 'col')), may hold values from -6 to 6
- conduction_bands: bfloat16 [256, 96, 9216], P(('row', 'col')), may hold values from -6 to 6
- valence_energy: float32 [256], P(('row', 'col')), may hold values from -8 to -0.5
- conduction_energy: float32 [256], P(('row', 'col')), may hold values from 0.5 to 8
- pair_valence: int32 [128, 4], P(('row', 'col')), may hold values from 0 to 1
- pair_conduction: int32 [128, 4], P(('row', 'col')), may hold values from 0 to 1
- pair_count: int32 [128], replicated, may hold values from 1 to 4, 256 in all
- stick_perm: int32 [160], replicated, may hold values from 0 to 159, each once
Outputs:
- response: float32 [20480, 20480], P('row', 'col')
Inputs may be any that keep to these rules, and one draw needn't show every extreme that they name: `pair_count`: the numbers sum to 256 and the largest is 4. `stick_perm`: A permutation of the box sticks.
All inputs are finite; a program needn't handle non-finite values.
Results may differ from a plain program's by a relative error of at most 0.0003.
Values sent between devices are 32-bit elements; how exact they have to be, the bound alone decides.
No kernel may reach another device: no remote copies, remote signals or barrier semaphores. Data moves between devices by JAX's collectives and lax.ppermute only.
A program may use at most 128 MiB of HBM per device.

v0:
```python
import math
import jax
import jax.numpy as jnp
from jax import lax
from jax.sharding import PartitionSpec as P

KX = 10
KY = 16
KZ = 64
CAP = 4
NPW = 20480


def transform(product):
    grid_size = product.shape[1]
    position = jnp.arange(grid_size, dtype=jnp.int32)

    def phases(frequency):
        return (frequency[:, None] * position[None, :] % grid_size).astype(jnp.float32) * (
            2.0 * math.pi / grid_size
        )

    x_phase = phases(jnp.arange(1, KX + 1, dtype=jnp.int32))
    y_phase = phases(jnp.arange(KY, dtype=jnp.int32))
    z_phase = phases(jnp.arange(KZ, dtype=jnp.int32))
    x_factor = jnp.concatenate([jnp.cos(x_phase), -jnp.sin(x_phase)], axis=0)
    x_section = jnp.einsum("gx,kxp->kgp", x_factor, product, precision=lax.Precision.HIGHEST)
    x_section = x_section.reshape(product.shape[0], 2 * KX, grid_size, grid_size)
    x_real = x_section[:, :KX]
    x_imag = x_section[:, KX:]
    y_cosine = jnp.cos(y_phase)
    y_sine = jnp.sin(y_phase)

    def along_y(factor_table, operand):
        return jnp.einsum("hy,kgyz->kghz", factor_table, operand, precision=lax.Precision.HIGHEST)

    y_real = along_y(y_cosine, x_real) + along_y(y_sine, x_imag)
    y_imag = along_y(y_cosine, x_imag) - along_y(y_sine, x_real)
    z_cosine = jnp.cos(z_phase).T
    z_sine = jnp.sin(z_phase).T

    def along_z(factor_table, operand):
        return jnp.einsum("kghz,zm->kghm", operand, factor_table, precision=lax.Precision.HIGHEST)

    z_real = along_z(z_cosine, y_real) + along_z(z_sine, y_imag)
    z_imag = along_z(z_cosine, y_imag) - along_z(z_sine, y_real)
    sticks = jnp.concatenate([z_real, z_imag], axis=-1) * grid_size ** (-1.5)
    return sticks.reshape(product.shape[0], KX * KY, 2 * KZ)


def body(
    valence_bands,
    conduction_bands,
    valence_energy,
    conduction_energy,
    pair_valence,
    pair_conduction,
    pair_count,
    stick_perm,
):
    row_devices = lax.axis_size("row")
    column_devices = lax.axis_size("col")
    devices = row_devices * column_devices
    self_index = lax.axis_index("row") * column_devices + lax.axis_index("col")
    slot_valence = pair_valence[0]
    slot_conduction = pair_conduction[0]
    live_slots = jnp.arange(CAP, dtype=jnp.int32) < pair_count[self_index]
    left_band = jnp.take(valence_bands, slot_valence, axis=0)
    right_band = jnp.take(conduction_bands, slot_conduction, axis=0)
    product = left_band.astype(jnp.float32) * right_band.astype(jnp.float32)
    sticks = transform(product)
    density = jnp.take(sticks, stick_perm, axis=1).reshape(CAP, NPW)
    weight = -1.0 / (
        jnp.take(conduction_energy, slot_conduction) - jnp.take(valence_energy, slot_valence)
    )
    weight = jnp.where(live_slots, weight, 0.0)
    weighted = density * weight[:, None]
    owned_width = NPW // devices
    row_side = weighted.reshape(CAP, devices, owned_width)
    column_side = (
        density.reshape(CAP, column_devices, row_devices, owned_width)
        .transpose(0, 2, 1, 3)
        .reshape(CAP, devices, owned_width)
    )
    row_pieces, column_pieces = (
        lax.all_to_all(row_side, ("row", "col"), split_axis=1, concat_axis=1, tiled=True),
        lax.all_to_all(column_side, ("row", "col"), split_axis=1, concat_axis=1, tiled=True),
    )
    row_received = row_pieces.reshape(CAP * devices, owned_width)
    column_received = column_pieces.reshape(CAP * devices, owned_width)
    column_panel = lax.all_gather(column_received, "row", axis=1, tiled=True)
    return lax.dot_general(
        lax.all_gather(row_received, "col", axis=1, tiled=True),
        column_panel,
        (((0,), (0,)), ((), ())),
        precision=lax.Precision.HIGHEST,
        preferred_element_type=jnp.float32,
    )


def solution(mesh):
    return jax.shard_map(
        body,
        mesh=mesh,
        in_specs=(
            P(("row", "col"), None, None),
            P(("row", "col"), None, None),
            P(("row", "col")),
            P(("row", "col")),
            P(("row", "col"), None),
            P(("row", "col"), None),
            P(),
            P(),
        ),
        out_specs=P("row", "col"),
        check_vma=False,
    )
```

profile of v0, /device:TPU:1, one launch (start us, length us, event | category | flops | bytes accessed | tf_op | source)
XLA Modules:
  0.0 219.2 jit_solution(10084126790357145682)
XLA Ops:
  13.1 4.0 %gather_fusion.1 = bf16[4,96,9216]{2,1,0:T(8,128)(2,1)} fusion(bf16[2,96,9216]{2,1,0:T(8,128)(2,1)S(1)} %copy-done, s32[1024]{0:T(1024)} %pad_clamp_fusion.2), kind=kCustom, calls=%fused_computation.clone | custom fusion | bytes 14155792 | tf_op jit(solution)/shard_map/jit(_take)/gather | solution.py:68
  17.2 6.1 %gather_fusion.2 = bf16[4,96,9216]{2,1,0:T(8,128)(2,1)} fusion(bf16[2,96,9216]{2,1,0:T(8,128)(2,1)} %param.13, s32[1024]{0:T(1024)} %pad_clamp_fusion.1), kind=kCustom, calls=%fused_computation.2.clone | custom fusion | bytes 14155792 | tf_op jit(solution)/shard_map/jit(_take)/gather | solution.py:69
  23.2 13.6 %fusion.4 = f32[4,20,9216]{2,1,0:T(8,128)} fusion(bf16[4,96,9216]{2,1,0:T(8,128)(2,1)} %gather_fusion.2, bf16[4,96,9216]{2,1,0:T(8,128)(2,1)} %gather_fusion.1, pred[4]{0:T(512)(128)(4,1)} %get-tuple-element.9, pred[4]{0:T(512)(128)(4,1)} %get-tuple-element.10, f32[10,96]{1,0:T(8,128)S(1)} %get-tuple-element.8, f32[10,96]{1,0:T(8,128)S(1)} %get-tuple-element.6), kind=kOutput, calls=%fused_computation.9 | convolution fusion | flops 867043200 | bytes 17112584 | tf_op jit(solution)/shard_map/gx,kxp->kgp/dot_general | solution.py:27
  36.8 4.3 %reshape.114 = f32[4,20,96,96]{3,2,1,0:T(8,128)} reshape(f32[4,20,9216]{2,1,0:T(8,128)} %fusion.4) | data formatting | bytes 5898240 | tf_op jit(solution)/shard_map/reshape | solution.py:28
  41.1 3.4 %fusion.53 = f32[4,10,96,16]{2,3,1,0:T(8,128)} fusion(f32[4,20,96,96]{3,2,1,0:T(8,128)} %reshape.114), kind=kOutput, calls=%fused_computation.62 | convolution fusion | flops 70792704 | bytes 3194880 | tf_op jit(solution)/shard_map/hy,kgyz->kghz/dot_general | solution.py:35
  44.6 3.4 %fusion.51 = f32[4,10,96,16]{2,3,1,0:T(8,128)} fusion(f32[4,20,96,96]{3,2,1,0:T(8,128)} %reshape.114), kind=kOutput, calls=%fused_computation.60 | convolution fusion | flops 70792704 | bytes 3194880 | tf_op jit(solution)/shard_map/hy,kgyz->kghz/dot_general | solution.py:35
  50.2 2.7 %fusion.13 = f32[4,10,16,96]{3,2,1,0:T(8,128)S(1)} fusion(f32[4,10,96,16]{2,3,1,0:T(8,128)} %fusion.53, f32[4,20,96,96]{3,2,1,0:T(8,128)} %reshape.114), kind=kOutput, calls=%fused_computation.20 | convolution fusion | flops 70854144 | bytes 3440640 | tf_op jit(solution)/shard_map/hy,kgyz->kghz/dot_general | solution.py:35
  53.5 2.7 %fusion.12 = f32[4,10,16,96]{3,2,1,0:T(8,128)S(1)} fusion(f32[4,10,96,16]{2,3,1,0:T(8,128)} %fusion.51, f32[4,20,96,96]{3,2,1,0:T(8,128)} %reshape.114), kind=kOutput, calls=%fused_computation.18 | convolution fusion | flops 70854144 | bytes 3440640 | tf_op jit(solution)/shard_map/hy,kgyz->kghz/dot_general | solution.py:35
  59.3 2.5 %gather_fusion = f32[160,4,128]{2,1,0:T(4,128)} fusion(f32[4,160,128]{2,0,1:T(4,128)} %maximum_multiply_fusion, s32[1024]{0:T(1024)S(1)} %pad_clamp_fusion), kind=kCustom, calls=%fused_computation.4 | custom fusion | bytes 656000 | tf_op jit(solution)/shard_map/jit(_take)/gather | solution.py:72
  61.9 1.7 copy.52
  63.6 2.0 gather.16
  67.2 24.8 %all_to_all.10 = f32[4,128,160]{2,0,1:T(4,128)} all-to-all(f32[4,128,160]{2,0,1:T(4,128)S(1)} %copy.58), channel_id=1, replica_groups=mesh['row'=8,'col'=16] {'row','col'}, dimensions={1} | all-to-all | bytes 655360 | tf_op jit(solution)/shard_map/all_to_all | solution.py:87
  92.0 2.0 copy.59
  94.0 1.7 copy.69
  97.3 2.0 gather.15
  101.3 1.5 copy.46
  102.8 2.0 copy.53
  107.3 1.8 select_multiply_fusion
  109.1 2.0 copy.54
  111.1 19.1 %all_to_all.11 = f32[4,128,160]{2,0,1:T(4,128)} all-to-all(f32[4,128,160]{2,0,1:T(4,128)} %copy.54), channel_id=1, replica_groups=mesh['row'=8,'col'=16] {'row','col'}, dimensions={1} | all-to-all | bytes 655360 | tf_op jit(solution)/shard_map/all_to_all | solution.py:86
  130.2 2.0 copy.55
  132.2 1.8 copy.70
  134.0 52.6 %all-gather.3.cloned.1.call-done = f32[512,2560]{0,1:T(8,128)} async-done(((f32[512,160]{0,1:T(8,128)}), f32[512,2560]{0,1:T(8,128)}) %all-gather.3.cloned.1.call-update) | async-done | bytes 5242896 | tf_op jit(solution)/shard_map/all_gather | solution.py:93
  186.5 25.8 %fusion.106 = f32[2560,1280]{1,0:T(8,128)} fusion(f32[512,2560]{0,1:T(8,128)} %all-gather.3.cloned.1.call-done, f32[512,1280]{0,1:T(8,128)} %all-gather.5.cloned.1.call-done), kind=kOutput, calls=%fused_computation.122 | convolution fusion | flops 20132659200 | bytes 20971520 | tf_op jit(solution)/shard_map/dot_general | solution.py:92
  (46 shorter events, 20.1 us)
Async XLA Ops:
  6.5 6.6 %copy-start = (bf16[2,96,9216]{2,1,0:T(8,128)(2,1)S(1)}, bf16[2,96,9216]{2,1,0:T(8,128)(2,1)}, u32[]{:S(2)}) copy-start(bf16[2,96,9216]{2,1,0:T(8,128)(2,1)} %param.12) | copy-start | bytes 10616836
  6.5 127.4 %all-gather.5.cloned.1.call-start = ((), (), s32[]{:S(2)}) async-start(), calls=%async_computation.3 | async-start | bytes 2949120 | tf_op jit(solution)/shard_map/all_gather | solution.py:91
  36.8 11.2 %copy-start.3 = (s32[160]{0:T(256)S(1)}, s32[160]{0:T(256)}, u32[]{:S(2)}) copy-start(s32[160]{0:T(256)} %compare_select_fusion) | copy-start | bytes 1924
  36.8 11.2 %copy-start.6 = (pred[160]{0:T(512)(128)(4,1)S(1)}, pred[160]{0:T(512)(128)(4,1)}, u32[]{:S(2)}) copy-start(pred[160]{0:T(512)(128)(4,1)} %compare_and_fusion.2) | copy-start | bytes 484
  58.1 41.2 %copy-start.1 = (f32[2]{0:T(128)S(1)}, f32[2]{0:T(128)}, u32[]{:S(2)}) copy-start(f32[2]{0:T(128)} %param.15) | copy-start | bytes 28
  58.3 42.3 %copy-start.2 = (f32[2]{0:T(128)S(1)}, f32[2]{0:T(128)}, u32[]{:S(2)}) copy-start(f32[2]{0:T(128)} %param.14) | copy-start | bytes 28
  61.8 44.2 %copy-start.4 = (s32[1,4]{1,0:T(1,128)S(1)}, s32[1,4]{1,0:T(1,128)}, u32[]{:S(2)}) copy-start(s32[1,4]{1,0:T(1,128)} %param.17) | copy-start | bytes 52
  61.9 44.2 %copy-start.5 = (s32[1,4]{1,0:T(1,128)S(1)}, s32[1,4]{1,0:T(1,128)}, u32[]{:S(2)}) copy-start(s32[1,4]{1,0:T(1,128)} %param.16) | copy-start | bytes 52
  95.8 90.8 %all-gather.3.cloned.1.call-start = ((), (), s32[]{:S(2)}) async-start(), calls=%async_computation.2 | async-start | bytes 5570560 | tf_op jit(solution)/shard_map/all_gather | solution.py:93
Sparse Core Ops, SparseCore 0:
  95.9 22.6 all-gather.4
  134.0 52.4 all-gather.2
where the time goes:
time: 220 us; the launch traced here: 219 us
  matrix products  53.9 us (24%)
  waiting for transfers between devices  52.6 us (24%)
  blocking collectives  44 us (20%)
  local copies, waits for them, and re-layouts  43.4 us (20%)
  between operations  13.5 us (6%)
  other arithmetic  11.7 us (5%)
    all_gather x1, waiting for transfers between devices, body(): lax.all_gather(row_received, 'col', axis=1, tiled=True)  52.6 us
    dot_general x1, matrix products, body(): lax.dot_general(lax.all_gather(row_received, 'col', axis=1, tiled=True),...  25.8 us
    all_to_all x1, blocking collectives, body(): lax.all_to_all(column_side, ('row', 'col'), split_axis=1, concat_axis=1,...  24.8 us
    all_to_all x1, blocking collectives, body(): lax.all_to_all(row_side, ('row', 'col'), split_axis=1, concat_axis=1, til...  19.1 us
    dot_general x1, matrix products, transform(): jnp.einsum('gx,kxp->kgp', x_factor, product, precision=lax.Precision.HIGH...  13.6 us
    dot_general x4, matrix products, along_y(): jnp.einsum('hy,kgyz->kghz', factor_table, operand, precision=lax.Precisio...  12.3 us
    gather x5, local copies, waits for them, and re-layouts, body(): density = jnp.take(sticks, stick_perm, axis=1).reshape(CAP, NPW)  10.3 us
    gather x1, local copies, waits for them, and re-layouts, body(): right_band = jnp.take(conduction_bands, slot_conduction, axis=0)  6.08 us
  transfers between devices with their start and end apart: 2, of which 1 were waited for; matrix products, arithmetic and copies ran while one was open for 9% of the time, Pallas kernels for 0%

commit v1 on v0

--- a/solution.py
+++ b/solution.py
@@ -9,6 +9,13 @@
 KZ = 64
 CAP = 4
 NPW = 20480
+
+
+def press_layers_all_over_axis(x_local):
+    local_part = tuple((x_local for _ in range(jax.lax.psum(1, axis_name="col"))))
+    then = jnp.stack(local_part, axis=0)
+    reached = jax.lax.all_to_all(then, axis_name="col", split_axis=0, concat_axis=0)
+    return jnp.concatenate(reached, 1)
 
 
 def transform(product):
@@ -90,7 +97,7 @@
     column_received = column_pieces.reshape(CAP * devices, owned_width)
     column_panel = lax.all_gather(column_received, "row", axis=1, tiled=True)
     return lax.dot_general(
-        lax.all_gather(row_received, "col", axis=1, tiled=True),
+        press_layers_all_over_axis(row_received),
         column_panel,
         (((0,), (0,)), ((), ())),
         precision=lax.Precision.HIGHEST,

time: 220 us -> 247 us (1.12); the launches traced: 219 us -> 243 us
  blocking collectives: 44 us -> 0 us
  waiting for transfers between devices: 52.6 us -> 92.2 us
  starting transfers between devices: 0.04 us -> 22.4 us
  local copies, waits for them, and re-layouts: 43.4 us -> 48.9 us
    all_to_all x0 -> x3, waiting for transfers between devices: none -> 65.6 us  [the longest x1 48.9 us: press_layers_all_over_axis(): jax.lax.all_to_all(then, axis_name='col', split_axis=0, concat_axis=0)]
    all_gather x1 -> x0, waiting for transfers between devices: 52.6 us -> none  [body(): lax.all_gather(row_received, 'col', axis=1, tiled=True)]
    all_to_all x2 -> x0, blocking collectives: 44 us -> none  [the longest x1 24.8 us: body(): lax.all_to_all(column_side, ('row', 'col'), split_axis=1, concat_axis=1,...]
    all_gather x1, waiting for transfers between devices: 0.02 us -> 26.6 us  [body(): column_panel = lax.all_gather(column_received, 'row', axis=1, tiled=True)]
    all_to_all x0 -> x3, starting transfers between devices: none -> 22.2 us  [the longest x1 11.9 us: body(): lax.all_to_all(row_side, ('row', 'col'), split_axis=1, concat_axis=1, til...]
    another operation x0 -> x1, local copies, waits for them, and re-layouts: none -> 4 us  [press_layers_all_over_axis(): then = jnp.stack(local_part, axis=0)]
  transfers between devices with their start and end apart: 2 -> 4, of which waited for: 1 -> 4; matrix products, arithmetic and copies ran while one was open for 9% -> 5% of each run, Pallas kernels for 0% -> 0%
where the time goes in v1:
time: 247 us; the launch traced here: 243 us
  waiting for transfers between devices  92.2 us (37%)
  matrix products  53.9 us (22%)
  local copies, waits for them, and re-layouts  48.9 us (20%)
  starting transfers between devices  22.4 us (9%)
  between operations  13.6 us (6%)
  other arithmetic  11.6 us (5%)
    all_to_all x1, waiting for transfers between devices, press_layers_all_over_axis(): jax.lax.all_to_all(then, axis_name='col', split_axis=0, concat_axis=0)  48.9 us
    all_gather x1, waiting for transfers between devices, body(): column_panel = lax.all_gather(column_received, 'row', axis=1, tiled=True)  26.6 us
    dot_general x1, matrix products, body(): lax.dot_general(press_layers_all_over_axis(row_received), column_panel, (...  25.8 us
    dot_general x1, matrix products, transform(): jnp.einsum('gx,kxp->kgp', x_factor, product, precision=lax.Precision.HIGH...  13.6 us
    dot_general x4, matrix products, along_y(): jnp.einsum('hy,kgyz->kghz', factor_table, operand, precision=lax.Precisio...  12.3 us
    all_to_all x1, starting transfers between devices, body(): lax.all_to_all(row_side, ('row', 'col'), split_axis=1, concat_axis=1, til...  11.9 us
    gather x5, local copies, waits for them, and re-layouts, body(): density = jnp.take(sticks, stick_perm, axis=1).reshape(CAP, NPW)  10.3 us
    all_to_all x1, waiting for transfers between devices, body(): lax.all_to_all(column_side, ('row', 'col'), split_axis=1, concat_axis=1,...  9.52 us
  transfers between devices with their start and end apart: 4, of which 4 were waited for; matrix products, arithmetic and copies ran while one was open for 5% of the time, Pallas kernels for 0%

profile of v1, /device:TPU:1, one launch (start us, length us, event | category | flops | bytes accessed | tf_op | source)
XLA Modules:
  0.0 242.7 jit_solution(5360992580952839506)
XLA Ops:
  13.0 4.0 %gather_fusion.1 = bf16[4,96,9216]{2,1,0:T(8,128)(2,1)} fusion(bf16[2,96,9216]{2,1,0:T(8,128)(2,1)S(1)} %copy-done, s32[1024]{0:T(1024)} %pad_clamp_fusion.2), kind=kCustom, calls=%fused_computation.clone | custom fusion | bytes 14155792 | tf_op jit(solution)/shard_map/jit(_take)/gather | solution.py:75
  17.0 6.1 %gather_fusion.2 = bf16[4,96,9216]{2,1,0:T(8,128)(2,1)} fusion(bf16[2,96,9216]{2,1,0:T(8,128)(2,1)} %param.13, s32[1024]{0:T(1024)} %pad_clamp_fusion.1), kind=kCustom, calls=%fused_computation.2.clone | custom fusion | bytes 14155792 | tf_op jit(solution)/shard_map/jit(_take)/gather | solution.py:76
  23.1 13.6 %fusion.4 = f32[4,20,9216]{2,1,0:T(8,128)} fusion(bf16[4,96,9216]{2,1,0:T(8,128)(2,1)} %gather_fusion.2, bf16[4,96,9216]{2,1,0:T(8,128)(2,1)} %gather_fusion.1, pred[4]{0:T(512)(128)(4,1)} %get-tuple-element.9, pred[4]{0:T(512)(128)(4,1)} %get-tuple-element.10, f32[10,96]{1,0:T(8,128)S(1)} %get-tuple-element.8, f32[10,96]{1,0:T(8,128)S(1)} %get-tuple-element.6), kind=kOutput, calls=%fused_computation.9 | convolution fusion | flops 867043200 | bytes 17112584 | tf_op jit(solution)/shard_map/gx,kxp->kgp/dot_general | solution.py:34
  36.7 4.3 %reshape.120 = f32[4,20,96,96]{3,2,1,0:T(8,128)} reshape(f32[4,20,9216]{2,1,0:T(8,128)} %fusion.4) | data formatting | bytes 5898240 | tf_op jit(solution)/shard_map/reshape | solution.py:35
  41.0 3.4 %fusion.53 = f32[4,10,96,16]{2,3,1,0:T(8,128)} fusion(f32[4,20,96,96]{3,2,1,0:T(8,128)} %reshape.120), kind=kOutput, calls=%fused_computation.62 | convolution fusion | flops 70792704 | bytes 3194880 | tf_op jit(solution)/shard_map/hy,kgyz->kghz/dot_general | solution.py:42
  44.5 3.4 %fusion.51 = f32[4,10,96,16]{2,3,1,0:T(8,128)} fusion(f32[4,20,96,96]{3,2,1,0:T(8,128)} %reshape.120), kind=kOutput, calls=%fused_computation.60 | convolution fusion | flops 70792704 | bytes 3194880 | tf_op jit(solution)/shard_map/hy,kgyz->kghz/dot_general | solution.py:42
  54.3 2.7 %fusion.13 = f32[4,10,16,96]{3,2,1,0:T(8,128)S(1)} fusion(f32[4,10,96,16]{2,3,1,0:T(8,128)} %fusion.53, f32[4,20,96,96]{3,2,1,0:T(8,128)} %reshape.120), kind=kOutput, calls=%fused_computation.20 | convolution fusion | flops 70854144 | bytes 3440640 | tf_op jit(solution)/shard_map/hy,kgyz->kghz/dot_general | solution.py:42
  57.6 2.7 %fusion.12 = f32[4,10,16,96]{3,2,1,0:T(8,128)S(1)} fusion(f32[4,10,96,16]{2,3,1,0:T(8,128)} %fusion.51, f32[4,20,96,96]{3,2,1,0:T(8,128)} %reshape.120), kind=kOutput, calls=%fused_computation.18 | convolution fusion | flops 70854144 | bytes 3440640 | tf_op jit(solution)/shard_map/hy,kgyz->kghz/dot_general | solution.py:42
  63.4 2.5 %gather_fusion = f32[160,4,128]{2,1,0:T(4,128)} fusion(f32[4,160,128]{2,0,1:T(4,128)} %maximum_multiply_fusion, s32[1024]{0:T(1024)S(1)} %pad_clamp_fusion), kind=kCustom, calls=%fused_computation.4 | custom fusion | bytes 656000 | tf_op jit(solution)/shard_map/jit(_take)/gather | solution.py:79
  67.7 2.0 gather.15
  69.7 2.0 copy.55
  76.0 2.0 copy.56
  78.0 11.9 %all-to-all-start = ((f32[4,128,160]{2,0,1:T(4,128)}), f32[4,128,160]{2,0,1:T(4,128)}, u32[]{:S(2)}, u32[]{:S(2)}) async-start(f32[4,128,160]{2,0,1:T(4,128)} %copy.56), calls=%async_computation | async-start | bytes 1048576 | tf_op jit(solution)/shard_map/all_to_all | solution.py:93
  91.4 2.0 gather.16
  95.8 7.2 %all-to-all-done = f32[4,128,160]{2,0,1:T(4,128)} async-done(((f32[4,128,160]{2,0,1:T(4,128)}), f32[4,128,160]{2,0,1:T(4,128)}, u32[]{:S(2)}, u32[]{:S(2)}) %all-to-all-start) | async-done | bytes 327712 | tf_op jit(solution)/shard_map/all_to_all | solution.py:93
  103.0 5.7 %all-to-all-start.2 = ((f32[4,128,160]{2,0,1:T(4,128)}), f32[4,128,160]{2,0,1:T(4,128)}, u32[]{:S(2)}, u32[]{:S(2)}) async-start(f32[4,128,160]{2,0,1:T(4,128)} %copy.60), calls=%async_computation.2 | async-start | bytes 1048576 | tf_op jit(solution)/shard_map/all_to_all | solution.py:94
  108.7 2.0 copy.57
  112.4 9.5 %all-to-all-done.2 = f32[4,128,160]{2,0,1:T(4,128)} async-done(((f32[4,128,160]{2,0,1:T(4,128)}), f32[4,128,160]{2,0,1:T(4,128)}, u32[]{:S(2)}, u32[]{:S(2)}) %all-to-all-start.2) | async-done | bytes 327712 | tf_op jit(solution)/shard_map/all_to_all | solution.py:94
  121.9 4.0 %stack.3 = f32[16,512,160]{1,2,0:T(8,128)} broadcast(f32[512,160]{0,1:T(8,128)} %bitcast.88), dimensions={1,2} | broadcast | bytes 5570560 | tf_op jit(solution)/shard_map/stack | solution.py:16
  125.9 4.6 %all-to-all-start.1 = ((f32[16,512,160]{1,2,0:T(8,128)}), f32[16,512,160]{1,2,0:T(8,128)}, u32[]{:S(2)}, u32[]{:S(2)}) async-start(f32[16,512,160]{1,2,0:T(8,128)} %stack.3), calls=%async_computation.1 | async-start | bytes 10485760 | tf_op jit(solution)/shard_map/all_to_all | solution.py:17
  130.7 2.0 copy.61
  134.5 26.6 %all-gather.2.cloned.1.call-done = f32[512,1280]{0,1:T(8,128)} async-done(((f32[512,160]{0,1:T(8,128)}), f32[512,1280]{0,1:T(8,128)}) %all-gather.2.cloned.1.call-update) | async-done | bytes 2621456 | tf_op jit(solution)/shard_map/all_gather | solution.py:98
  161.1 48.9 %all-to-all-done.1 = f32[16,512,160]{1,2,0:T(8,128)} async-done(((f32[16,512,160]{1,2,0:T(8,128)}), f32[16,512,160]{1,2,0:T(8,128)}, u32[]{:S(2)}, u32[]{:S(2)}) %all-to-all-start.1) | async-done | bytes 5242912 | tf_op jit(solution)/shard_map/all_to_all | solution.py:17
  210.0 25.8 %fusion.106 = f32[2560,1280]{1,0:T(8,128)} fusion(f32[512,2560]{0,1:T(8,128)} %bitcast.23, f32[512,1280]{0,1:T(8,128)} %all-gather.2.cloned.1.call-done), kind=kOutput, calls=%fused_computation.122 | convolution fusion | flops 20132659200 | bytes 20971520 | tf_op jit(solution)/shard_map/dot_general | solution.py:99
  (46 shorter events, 30.2 us)
Async XLA Ops:
  6.5 6.5 %copy-start = (bf16[2,96,9216]{2,1,0:T(8,128)(2,1)S(1)}, bf16[2,96,9216]{2,1,0:T(8,128)(2,1)}, u32[]{:S(2)}) copy-start(bf16[2,96,9216]{2,1,0:T(8,128)(2,1)} %param.12) | copy-start | bytes 10616836
  36.7 11.2 %copy-start.3 = (s32[160]{0:T(256)S(1)}, s32[160]{0:T(256)}, u32[]{:S(2)}) copy-start(s32[160]{0:T(256)} %compare_select_fusion) | copy-start | bytes 1924
  36.7 11.2 %copy-start.1 = (f32[2]{0:T(128)S(1)}, f32[2]{0:T(128)}, u32[]{:S(2)}) copy-start(f32[2]{0:T(128)} %param.15) | copy-start | bytes 28
  36.7 12.0 %copy-start.2 = (f32[2]{0:T(128)S(1)}, f32[2]{0:T(128)}, u32[]{:S(2)}) copy-start(f32[2]{0:T(128)} %param.14) | copy-start | bytes 28
  57.5 15.3 %copy-start.4 = (s32[1,4]{1,0:T(1,128)S(1)}, s32[1,4]{1,0:T(1,128)}, u32[]{:S(2)}) copy-start(s32[1,4]{1,0:T(1,128)} %param.17) | copy-start | bytes 52
  57.5 15.3 %copy-start.5 = (s32[1,4]{1,0:T(1,128)S(1)}, s32[1,4]{1,0:T(1,128)}, u32[]{:S(2)}) copy-start(s32[1,4]{1,0:T(1,128)} %param.16) | copy-start | bytes 52
  78.0 25.0 %all-to-all-start = ((f32[4,128,160]{2,0,1:T(4,128)}), f32[4,128,160]{2,0,1:T(4,128)}, u32[]{:S(2)}, u32[]{:S(2)}) async-start(f32[4,128,160]{2,0,1:T(4,128)} %copy.56), calls=%async_computation | async-start | bytes 1048576 | tf_op jit(solution)/shard_map/all_to_all | solution.py:93
  103.0 18.9 %all-to-all-start.2 = ((f32[4,128,160]{2,0,1:T(4,128)}), f32[4,128,160]{2,0,1:T(4,128)}, u32[]{:S(2)}, u32[]{:S(2)}) async-start(f32[4,128,160]{2,0,1:T(4,128)} %copy.60), calls=%async_computation.2 | async-start | bytes 1048576 | tf_op jit(solution)/shard_map/all_to_all | solution.py:94
  125.9 84.1 %all-to-all-start.1 = ((f32[16,512,160]{1,2,0:T(8,128)}), f32[16,512,160]{1,2,0:T(8,128)}, u32[]{:S(2)}, u32[]{:S(2)}) async-start(f32[16,512,160]{1,2,0:T(8,128)} %stack.3), calls=%async_computation.1 | async-start | bytes 10485760 | tf_op jit(solution)/shard_map/all_to_all | solution.py:17
  130.5 30.6 %all-gather.2.cloned.1.call-start = ((), (), s32[]{:S(2)}) async-start(), calls=%async_computation.3 | async-start | bytes 2949120 | tf_op jit(solution)/shard_map/all_gather | solution.py:98
Sparse Core Ops, SparseCore 0:
  134.6 26.4 all-gather.1
